TPU v7x, 256 devices: a whole 4x4x8 slice. The times are simulated.
256 devices in a mesh: row: 16 (over x, y), col: 16 (over z, core).
Axes of the slice: x: 4, y: 4, z: 8, core: 2. Of those that a mesh axis runs over, the one named last changes fastest.
Arguments:
- start_block: float32 [65536, 128], P(('row', 'col')), may hold values from -6 to 6
- vertex_scale: float32 [65536], P(('row', 'col')), may hold values from 0.015625 to 0.0625
- adj_tiles: bfloat16 [16, 16, 64, 128, 128], P('row', 'col'), may hold values from 0 to 1
- tile_row: int32 [16, 16, 64], P('row', 'col'), may hold values from 0 to 31
- tile_col: int32 [16, 16, 64], P('row', 'col'), may hold values from 0 to 31
- live_count: int32 [16, 16], P('row', 'col'), may hold values from 16 to 64, as said below
- rotation_first: float32 [256, 128], replicated, may hold values from -0.375 to 0.375
- rotation_second: float32 [384, 128], replicated, may hold values from -0.3125 to 0.3125
Outputs:
- final_block: float32 [65536, 128], P(('row', 'col'))
- final_image: float32 [65536, 128], P(('row', 'col'))
Inputs may be any that keep to these rules, and one draw needn't show every extreme that they name: Slots from live_count on are ignored; at least one device has all 64 slots live in every draw.
All inputs are finite; a program needn't handle non-finite values.
Results may differ from a plain program's by a relative error of at most 0.01.
Values may be sent and summed in bfloat16 or wider, within the bound.
A program may use at most 64 MiB of HBM per device.

v0:
```python
import jax
import jax.numpy as jnp
from jax import lax
from jax.sharding import PartitionSpec as P

HIGH = lax.Precision.HIGHEST


def tile_products(tiles_here, cols_here, count_here, flat_panel, span_slots, tile_side, width_k):
    alive_mask = jnp.arange(span_slots, dtype=jnp.int32) < count_here
    pieces = jnp.take(flat_panel, cols_here, axis=0)
    pieces = jnp.where(alive_mask[:, None], pieces, jnp.zeros_like(pieces))
    pieces = pieces.reshape(span_slots, tile_side, width_k)
    tile_out = jnp.einsum("tab,tbk->tak", tiles_here, pieces, preferred_element_type=jnp.float32)
    return tile_out.reshape(span_slots, tile_side * width_k)


def place_rows(rows_slot, tile_out, row_tiles, tile_side, width_k):
    placed = jax.ops.segment_sum(tile_out, rows_slot, num_segments=row_tiles)
    return placed.reshape(row_tiles * tile_side, width_k)


def apply_operator(block, vertex_scale, tiles_here, rows_here, cols_here, count_here):
    tile_side = tiles_here.shape[-1]
    width_k = block.shape[1]
    slot_total = tiles_here.shape[0]
    scaled = (vertex_scale[:, None] * block).astype(jnp.bfloat16)
    gathered = lax.all_gather(scaled, "col", axis=0, tiled=True)
    flat_panel = gathered.reshape(gathered.shape[0] // tile_side, tile_side * width_k)
    row_tiles = lax.axis_size("row") * block.shape[0] // tile_side
    tile_out = tile_products(
        tiles_here, cols_here, count_here, flat_panel, slot_total, tile_side, width_k
    )
    partial_value = place_rows(rows_here, tile_out, row_tiles, tile_side, width_k)
    summed = lax.psum_scatter(
        partial_value.astype(jnp.bfloat16), "row", scatter_dimension=0, tiled=True
    ).astype(jnp.float32)
    return block - vertex_scale[:, None] * summed


def inner(left, right):
    return jnp.einsum("sk,sl->kl", left, right, precision=HIGH)


def residual_block(block, image, verts_all):
    gram = lax.psum(inner(block, image), ("row", "col")) / verts_all
    resid = image - jnp.dot(block, gram, precision=HIGH)
    colsq = lax.psum(jnp.sum(resid * resid, axis=0), ("row", "col"))
    return resid * lax.rsqrt(colsq / verts_all + 1e-06)


def local(
    start_block,
    vertex_scale,
    adj_tiles,
    tile_row,
    tile_col,
    live_count,
    rotation_first,
    rotation_second,
):
    width_k = start_block.shape[1]
    verts_all = start_block.shape[0] * lax.axis_size("row") * lax.axis_size("col")
    tiles_here = adj_tiles[0, 0]
    rows_here = tile_row[0, 0]
    cols_here = tile_col[0, 0]
    count_here = live_count[0, 0]

    def oper(block):
        return apply_operator(block, vertex_scale, tiles_here, rows_here, cols_here, count_here)

    image0 = oper(start_block)
    search0 = residual_block(start_block, image0, verts_all)
    simage0 = oper(search0)
    rot_x, rot_w = (rotation_first[:width_k], rotation_first[width_k:])
    block1 = jnp.dot(start_block, rot_x, precision=HIGH) + jnp.dot(search0, rot_w, precision=HIGH)
    image1 = jnp.dot(image0, rot_x, precision=HIGH) + jnp.dot(simage0, rot_w, precision=HIGH)
    prev1 = jnp.dot(search0, rot_w, precision=HIGH)
    pimage1 = jnp.dot(simage0, rot_w, precision=HIGH)
    search1 = residual_block(block1, image1, verts_all)
    simage1 = oper(search1)
    rot_qx = rotation_second[:width_k]
    rot_qw = rotation_second[width_k : 2 * width_k]
    rot_qp = rotation_second[2 * width_k :]
    final_block = (
        jnp.dot(block1, rot_qx, precision=HIGH)
        + jnp.dot(search1, rot_qw, precision=HIGH)
        + jnp.dot(prev1, rot_qp, precision=HIGH)
    )
    final_image = (
        jnp.dot(image1, rot_qx, precision=HIGH)
        + jnp.dot(simage1, rot_qw, precision=HIGH)
        + jnp.dot(pimage1, rot_qp, precision=HIGH)
    )
    return (final_block, final_image)


def solution(mesh):
    placed = (
        P(("row", "col"), None),
        P(("row", "col")),
        P("row", "col", None, None, None),
        P("row", "col", None),
        P("row", "col", None),
        P("row", "col"),
        P(),
        P(),
    )
    return jax.shard_map(
        local,
        mesh=mesh,
        in_specs=placed,
        out_specs=(P(("row", "col"), None), P(("row", "col"), None)),
        check_vma=False,
    )
```

profile of v0, /device:TPU:1, one launch (start us, length us, event | category | flops | bytes accessed | tf_op | source)
XLA Modules:
  0.0 1100.2 jit_solution(16218495195349804594)
XLA Ops:
  7.2 1.1 copy.23
  8.4 1.3 multiply_convert_fusion.2
  10.4 0.7 compare_select_fusion
  11.1 0.7 compare_and_fusion
  11.7 40.5 %all-gather.4.cloned.1.call-done = bf16[4096,128]{0,1:T(8,128)(2,1)} async-done(((bf16[256,128]{0,1:T(8,128)(2,1)}), bf16[4096,128]{0,1:T(8,128)(2,1)}) %all-gather.4.cloned.1.call-update) | async-done | bytes 1048592 | tf_op jit(solution)/shard_map/all_gather | solution.py:28
  52.2 2.3 copy.19
  54.5 1.5 reshape.49
  56.0 3.2 gather_fusion
  59.2 1.9 fusion.14
  61.1 0.6 copy.40
  61.7 3.6 convolution_bitcast_fusion.2
  65.3 5.6 copy.21
  70.9 10.6 scatter_custom_fusion
  81.5 1.7 convert_element_type.37
  83.2 1.3 convert_element_type.38
  84.5 2.3 copy.22
  86.9 75.2 %reduce-scatter.4.cloned.1.call-done = bf16[256,128]{0,1:T(8,128)(2,1)} async-done(((bf16[4096,128]{0,1:T(8,128)(2,1)}), bf16[256,128]{0,1:T(8,128)(2,1)}) %reduce-scatter.4.cloned.1.call-update) | async-done | bytes 65552 | tf_op jit(solution)/shard_map/reduce_scatter | solution.py:35
  162.0 1.7 convolution_bitcast_fusion.4
  163.9 244.3 %all-reduce.3.cloned.1.call-done = f32[128,128]{0,1:T(8,128)} async-done(((f32[128,128]{0,1:T(8,128)}), f32[128,128]{0,1:T(8,128)}) %all-reduce.3.cloned.1.call-update) | async-done | bytes 65552 | tf_op jit(solution)/shard_map/psum | solution.py:46
  408.2 1.2 multiply_reduce_fusion.1
  409.4 74.4 %psum.29 = f32[128]{0:T(128)S(1)} all-reduce(f32[128]{0:T(128)S(1)} %get-tuple-element.3), channel_id=1, replica_groups=mesh['row'=16,'col'=16] {'row','col'}, use_global_device_ids=true, to_apply=%region_4.6 | all-reduce | flops 128 | bytes 1024 | tf_op jit(solution)/shard_map/psum | solution.py:48
  483.9 0.5 copy-done.12
  484.4 0.7 multiply_convert_fusion.1
  485.3 32.4 %all-gather.6.cloned.1.call-done = bf16[4096,128]{0,1:T(8,128)(2,1)} async-done(((bf16[256,128]{0,1:T(8,128)(2,1)}), bf16[4096,128]{0,1:T(8,128)(2,1)}) %all-gather.6.cloned.1.call-update) | async-done | bytes 1048592 | tf_op jit(solution)/shard_map/all_gather | solution.py:28
  517.7 2.3 copy.24
  520.0 1.5 reshape.52
  521.5 3.2 gather_fusion.1
  524.7 1.9 fusion.13
  526.6 0.6 copy.42
  527.2 3.6 convolution_bitcast_fusion.1
  530.8 5.6 copy.26
  536.4 10.6 scatter_custom_fusion.1
  547.0 1.7 convert_element_type.41
  548.7 1.3 convert_element_type.42
  550.0 2.3 copy.27
  552.6 0.5 fusion.29
  553.1 0.3 convolution_add_fusion.5
  553.4 74.1 %reduce-scatter.6.cloned.1.call-done = bf16[256,128]{0,1:T(8,128)(2,1)} async-done(((bf16[4096,128]{0,1:T(8,128)(2,1)}), bf16[256,128]{0,1:T(8,128)(2,1)}) %reduce-scatter.6.cloned.1.call-update) | async-done | bytes 65552 | tf_op jit(solution)/shard_map/reduce_scatter | solution.py:35
  627.5 1.3 fusion.22
  628.8 0.6 copy-done.6
  629.5 0.3 convolution_add_fusion.4
  629.9 0.9 fusion.55
  630.8 241.1 %all-reduce.5.cloned.1.call-done = f32[128,128]{0,1:T(8,128)} async-done(((f32[128,128]{0,1:T(8,128)}), f32[128,128]{0,1:T(8,128)}) %all-reduce.5.cloned.1.call-update) | async-done | bytes 65552 | tf_op jit(solution)/shard_map/psum | solution.py:46
  871.9 1.2 multiply_reduce_fusion
  873.1 74.4 %psum.31 = f32[128]{0:T(128)S(1)} all-reduce(f32[128]{0:T(128)S(1)} %get-tuple-element.5), channel_id=1, replica_groups=mesh['row'=16,'col'=16] {'row','col'}, use_global_device_ids=true, to_apply=%region_9.11 | all-reduce | flops 128 | bytes 1024 | tf_op jit(solution)/shard_map/psum | solution.py:48
  947.6 0.7 multiply_convert_fusion
  948.4 32.6 %all-gather.8.cloned.1.call-done = bf16[4096,128]{0,1:T(8,128)(2,1)} async-done(((bf16[256,128]{0,1:T(8,128)(2,1)}), bf16[4096,128]{0,1:T(8,128)(2,1)}) %all-gather.8.cloned.1.call-update) | async-done | bytes 1048592 | tf_op jit(solution)/shard_map/all_gather | solution.py:28
  980.9 2.3 copy.31
  983.2 1.5 reshape.55
  984.7 3.2 gather_fusion.2
  987.9 1.9 fusion.12
  989.8 0.6 copy.44
  990.4 3.6 convolution_bitcast_fusion
  994.0 5.6 copy.33
  999.6 10.6 scatter_custom_fusion.2
  1010.2 1.7 convert_element_type.45
  1011.9 1.3 convert_element_type.46
  1013.2 2.3 copy.34
  1015.9 0.4 fusion.43
  1016.2 0.5 convolution_add_fusion.3
  1016.7 0.9 convolution_add_fusion.2
  1017.6 73.1 %reduce-scatter.8.cloned.1.call-done = bf16[256,128]{0,1:T(8,128)(2,1)} async-done(((bf16[4096,128]{0,1:T(8,128)(2,1)}), bf16[256,128]{0,1:T(8,128)(2,1)}) %reduce-scatter.8.cloned.1.call-update) | async-done | bytes 65552 | tf_op jit(solution)/shard_map/reduce_scatter | solution.py:35
  1090.7 1.3 convolution_add_fusion.1
  1092.1 0.9 convolution_add_fusion
  (47 shorter events, 1.3 us)
Async XLA Ops:
  7.2 54.5 %copy-start = (bf16[1,1,64,128,128]{4,3,2,1,0:T(8,128)(2,1)S(1)}, bf16[1,1,64,128,128]{4,3,2,1,0:T(8,128)(2,1)}, u32[]{:S(2)}) copy-start(bf16[1,1,64,128,128]{4,3,2,1,0:T(8,128)(2,1)} %param.12) | copy-start | bytes 6291460
  7.2 45.0 %all-gather.4.cloned.1.call-start = ((), (), s32[]{:S(2)}) async-start(), calls=%async_computation.3 | async-start | bytes 1114112 | tf_op jit(solution)/shard_map/all_gather | solution.py:28
  9.7 152.3 %reduce-scatter.4.cloned.1.call-start = ((), (), s32[]{:S(2)}) async-start(), calls=%async_computation.4 | async-start | bytes 1114112 | tf_op jit(solution)/shard_map/reduce_scatter | solution.py:35
  84.5 77.5 %copy-start.1 = (f32[256,128]{1,0:T(8,128)S(1)}, f32[256,128]{1,0:T(8,128)}, u32[]{:S(2)}) copy-start(f32[256,128]{1,0:T(8,128)} %param.10) | copy-start | bytes 393220
  84.5 77.5 %copy-start.11 = (f32[256]{0:T(256)S(1)}, f32[256]{0:T(256)}, u32[]{:S(2)}) copy-start(f32[256]{0:T(256)} %param.11) | copy-start | bytes 3076
  86.8 321.4 %all-reduce.3.cloned.1.call-start = ((), (), s32[]{:S(2)}) async-start(), calls=%async_computation.5 | async-start | bytes 131072 | tf_op jit(solution)/shard_map/psum | solution.py:46
  163.8 353.9 %all-gather.6.cloned.1.call-start = ((), (), s32[]{:S(2)}) async-start(), calls=%async_computation.6 | async-start | bytes 1114112 | tf_op jit(solution)/shard_map/all_gather | solution.py:28
  483.9 0.5 copy-start.12
  485.1 142.4 %reduce-scatter.6.cloned.1.call-start = ((), (), s32[]{:S(2)}) async-start(), calls=%async_computation.7 | async-start | bytes 1114112 | tf_op jit(solution)/shard_map/reduce_scatter | solution.py:35
  550.0 2.6 copy-start.10
  550.0 2.6 copy-start.13
  550.0 79.5 %copy-start.9 = (bf16[256,128]{0,1:T(8,128)(2,1)S(1)}, bf16[256,128]{0,1:T(8,128)(2,1)}, u32[]{:S(2)}) copy-start(bf16[256,128]{0,1:T(8,128)(2,1)} %reduce-scatter.4.cloned.1.call-done) | copy-start | bytes 196612
  552.3 319.6 %all-reduce.5.cloned.1.call-start = ((), (), s32[]{:S(2)}) async-start(), calls=%async_computation.8 | async-start | bytes 131072 | tf_op jit(solution)/shard_map/psum | solution.py:46
  553.1 427.8 %copy-start.4 = (f32[256,128]{1,0:T(8,128)}, f32[256,128]{1,0:T(8,128)S(1)}, u32[]{:S(2)}) copy-start(f32[256,128]{1,0:T(8,128)S(1)} %fusion.29) | copy-start | bytes 393220
  553.4 427.6 %copy-start.2 = (f32[256,128]{1,0:T(8,128)}, f32[256,128]{1,0:T(8,128)S(1)}, u32[]{:S(2)}) copy-start(f32[256,128]{1,0:T(8,128)S(1)} %convolution_add_fusion.5) | copy-start | bytes 393220
  628.8 0.6 copy-start.6
  630.8 350.1 %all-gather.8.cloned.1.call-start = ((), (), s32[]{:S(2)}) async-start(), calls=%async_computation.9 | async-start | bytes 1114112 | tf_op jit(solution)/shard_map/all_gather | solution.py:28
  948.3 142.4 %reduce-scatter.8.cloned.1.call-start = ((), (), s32[]{:S(2)}) async-start(), calls=%async_computation.10 | async-start | bytes 1114112 | tf_op jit(solution)/shard_map/reduce_scatter | solution.py:35
  1013.2 2.3 copy-start.3
  1013.2 2.4 copy-start.8
  1013.2 3.5 copy-start.5
  1015.5 76.5 %copy-start.7 = (f32[256,128]{1,0:T(8,128)S(1)}, f32[256,128]{1,0:T(8,128)}, u32[]{:S(2)}) copy-start(f32[256,128]{1,0:T(8,128)} %copy-done.6) | copy-start | bytes 393220
Sparse Core Ops, SparseCore 0:
  10.3 41.8 all-gather.3
  87.0 75.0 reduce-scatter.3
  169.0 239.1 all-reduce.2
  485.2 32.4 all-gather.5
  552.5 74.9 reduce-scatter.5
  632.9 239.0 all-reduce.4
  948.4 32.4 all-gather.7
  1015.7 75.0 reduce-scatter.7
where the time goes:
time: 1110 us; the launch traced here: 1100 us
  waiting for transfers between devices  813 us (73%)
  blocking collectives  149 us (13%)
  local copies, waits for them, and re-layouts  52.7 us (5%)
  other arithmetic  46.7 us (4%)
  matrix products  22.4 us (2%)
  between operations  15.4 us (1%)
    psum x2, waiting for transfers between devices, residual_block(): gram = lax.psum(inner(block, image), ('row', 'col')) / verts_all  485 us
    reduce_scatter x3, waiting for transfers between devices, apply_operator(): lax.psum_scatter(partial_value.astype(jnp.bfloat16), 'row', scatter_dimen...  222 us
    psum x2, blocking collectives, residual_block(): colsq = lax.psum(jnp.sum(resid * resid, axis=0), ('row', 'col'))  149 us
    all_gather x3, waiting for transfers between devices, apply_operator(): gathered = lax.all_gather(scaled, 'col', axis=0, tiled=True)  105 us
    scatter-add x3, other arithmetic, place_rows(): placed = jax.ops.segment_sum(tile_out, rows_slot, num_segments=row_tiles)  31.9 us
  transfers between devices with their start and end apart: 8, of which 8 were waited for; matrix products, arithmetic and copies ran while one was open for 0% of the time, Pallas kernels for 0%

commit v1 on v0

v1 whole, which is shorter than its diff:
```python
import jax
import jax.numpy as jnp
from jax import lax
from jax.experimental import pallas as pl
from jax.experimental.pallas import tpu as pltpu
from jax.sharding import PartitionSpec as P

MESH = pl.DeviceIdType.MESH
HIGH = lax.Precision.HIGHEST
F32 = jnp.float32
BF16 = jnp.bfloat16
T = 128
SLOTS = 64
VERTS = 65536
OPS = 3


def mm(left, right):
    return jnp.dot(left, right, precision=HIGH, preferred_element_type=F32)


def gram_of(left, right):
    return lax.dot_general(
        left, right, (((0,), (0,)), ((), ())), precision=HIGH, preferred_element_type=F32
    )


def kernel(
    x_ref, scale_ref, tiles_hbm, rows_ref, cols_ref, live_ref, rot1_ref, rot2_ref,
    block_ref, image_ref,
    tiles, panel_0, panel_1, panel_2, running, index_v, index_s, s_b, d0_ref, x1_ref, d1_ref, p1_ref, dp1_ref, part,
    send_x, send_y, recv_x, recv_y, mid_x, mid_y, last_x, last_y,
    pay, red_a, got_a, red_b, got_s, got_b, got_c,
    tile_sem, index_sem, ag_send, ag_recv, rs_send, rs_recv, ar_send, ar_recv,
):
    panels = (panel_0, panel_1, panel_2)
    r = lax.axis_index("row")
    c = lax.axis_index("col")
    x, y = r // 4, lax.rem(r, 4)
    z, k = c // 2, lax.rem(c, 2)
    sib = c + 1 - 2 * k

    def along_x(step):
        return (lax.rem(x + step, 4) * 4 + y, c)

    def along_y(step):
        return (x * 4 + lax.rem(y + step, 4), c)

    def along_z(step):
        return (r, lax.rem(z + step + 8, 8) * 2 + k)

    def send(src, dst, send_sem, recv_sem, device):
        pltpu.make_async_remote_copy(
            src_ref=src, dst_ref=dst, send_sem=send_sem, recv_sem=recv_sem,
            device_id=device, device_id_type=MESH,
        ).start()

    def wait(ref, sem):
        pltpu.make_async_copy(ref, ref, sem).wait()

    tile_copy = pltpu.make_async_copy(tiles_hbm, tiles, tile_sem)
    tile_copy.start()

    barrier = pltpu.get_barrier_semaphore()

    def greet_row(step, carry):
        pl.semaphore_signal(
            barrier, inc=1, device_id=(lax.rem(r + step, 16), c), device_id_type=MESH
        )
        return carry

    def greet_z(step, carry):
        pl.semaphore_signal(barrier, inc=1, device_id=along_z(step), device_id_type=MESH)
        return carry

    pl.semaphore_signal(barrier, inc=1, device_id=(r, sib), device_id_type=MESH)
    lax.fori_loop(1, 8, greet_z, 0)
    lax.fori_loop(1, 16, greet_row, 0)

    lane = lax.broadcasted_iota(jnp.int32, (T, T), 1)
    sub = lax.broadcasted_iota(jnp.int32, (T, T), 0)
    eye = (lane == sub).astype(F32)
    for half in range(2):
        column = jnp.sum(eye * scale_ref[pl.ds(half, 1), :], axis=1, keepdims=True)
        s_b[pl.ds(half * T, T), :] = jnp.broadcast_to(column, (T, T))

    mine = (k * 8 + z) * 2

    def put_block(op, value):
        scaled = (s_b[...] * value).astype(BF16)
        panels[op][mine] = scaled[:T]
        panels[op][mine + 1] = scaled[T:]

    def at_z(step):
        return (k * 8 + lax.rem(z + step + 8, 8)) * 2

    def gather_start(op):
        own = panels[op].at[pl.ds(mine, 2)]
        send(own, own, ag_send.at[op], ag_recv.at[op, 1], along_z(2))
        send(own, own, ag_send.at[op], ag_recv.at[op, 2], along_z(-2))
        send(own, own, ag_send.at[op], ag_recv.at[op, 3], along_z(1))
        send(own, own, ag_send.at[op], ag_recv.at[op, 4], along_z(-1))
        send(own, own, ag_send.at[op], ag_recv.at[op, 0], (r, sib))

    def to_sibling(op, step):
        block = panels[op].at[pl.ds(at_z(step), 2)]
        send(block, block, ag_send.at[op], ag_recv.at[op, 0], (r, sib))

    def gather_middle(op):
        up = panels[op].at[pl.ds(at_z(-2), 2)]
        low = panels[op].at[pl.ds(at_z(-2), 1)]
        wait(up, ag_recv.at[op, 1])
        send(low, low, ag_send.at[op], ag_recv.at[op, 5], along_z(2))
        send(up, up, ag_send.at[op], ag_recv.at[op, 6], along_z(1))
        down = panels[op].at[pl.ds(at_z(2), 2)]
        high = panels[op].at[pl.ds(at_z(2) + 1, 1)]
        wait(down, ag_recv.at[op, 2])
        send(high, high, ag_send.at[op], ag_recv.at[op, 7], along_z(-2))
        send(down, down, ag_send.at[op], ag_recv.at[op, 8], along_z(-1))
        to_sibling(op, -2)
        to_sibling(op, 2)
        wait(panels[op].at[pl.ds(at_z(-1), 2)], ag_recv.at[op, 3])
        to_sibling(op, -1)
        wait(panels[op].at[pl.ds(at_z(1), 2)], ag_recv.at[op, 4])
        to_sibling(op, 1)

    def gather_end(op):
        wait(panels[op].at[pl.ds(at_z(-3), 2)], ag_recv.at[op, 6])
        to_sibling(op, -3)
        wait(panels[op].at[pl.ds(at_z(3), 2)], ag_recv.at[op, 8])
        to_sibling(op, 3)
        wait(panels[op].at[pl.ds(at_z(4), 1)], ag_recv.at[op, 5])
        wait(panels[op].at[pl.ds(at_z(4) + 1, 1)], ag_recv.at[op, 7])
        to_sibling(op, 4)
        wait(panels[op].at[pl.ds((1 - k) * 16, 16)], ag_recv.at[op, 0])

    def products(op):
        def slot(t, total):
            product = jnp.dot(
                tiles[index_s[0, t]], panels[op][index_s[1, t]], preferred_element_type=F32
            )
            total = jnp.where(index_s[2, t] > 0, product, total + product)
            running[t] = total
            return total

        lax.fori_loop(0, SLOTS, slot, jnp.zeros((T, T), F32), unroll=8)

    def scatter_start(op):
        for step in (1, 3, 2, 0):
            for other in range(4):
                tile = (lax.rem(x + step, 4) * 4 + other) * 2
                send_x[op, step, other] = running[index_s[3, tile]].astype(BF16)
            if step:
                send(send_x.at[op, step], recv_x.at[op, step - 1],
                     rs_send.at[op, 0], rs_recv.at[op, 0], along_x(step))
            for other in range(4):
                tile = (other * 4 + lax.rem(y + step, 4)) * 2 + 1
                send_y[op, step, other] = running[index_s[3, tile]].astype(BF16)
            if step:
                send(send_y.at[op, step], recv_y.at[op, step - 1],
                     rs_send.at[op, 0], rs_recv.at[op, 1], along_y(step))

    def sum_of(own, got, op, at):
        return (
            own[op, 0, at].astype(F32) + got[op, 0, at].astype(F32)
            + got[op, 1, at].astype(F32) + got[op, 2, at].astype(F32)
        )

    def scatter_middle(op):
        wait(recv_x.at[op], rs_recv.at[op, 0])
        for step in (1, 3, 2):
            mid_x[op, step - 1] = sum_of(send_x, recv_x, op, lax.rem(y + step, 4)).astype(BF16)
            send(mid_x.at[op, step - 1], last_x.at[op, step - 1],
                 rs_send.at[op, 1], rs_recv.at[op, 2], along_y(step))
        wait(recv_y.at[op], rs_recv.at[op, 1])
        for step in (1, 3, 2):
            mid_y[op, step - 1] = sum_of(send_y, recv_y, op, lax.rem(x + step, 4)).astype(BF16)
            send(mid_y.at[op, step - 1], last_y.at[op, step - 1],
                 rs_send.at[op, 1], rs_recv.at[op, 3], along_x(step))
        part[pl.ds(0, T), :] = sum_of(send_x, recv_x, op, y)
        part[pl.ds(T, T), :] = sum_of(send_y, recv_y, op, x)

    def scatter_end(op):
        def total(last):
            return (
                last[op, 0].astype(F32) + last[op, 1].astype(F32) + last[op, 2].astype(F32)
            )

        wait(last_x.at[op], rs_recv.at[op, 2])
        part[pl.ds(0, T), :] += total(last_x)
        wait(last_y.at[op], rs_recv.at[op, 3])
        part[pl.ds(T, T), :] += total(last_y)
        return -(s_b[...] * part[...])

    def reduce_start(g, xd, dd):
        pay[g, :, pl.ds(8, 8), :] = xd.reshape(16, 8, T)
        pay[g, :, pl.ds(16, 8), :] = dd.reshape(16, 8, T)

        def one(step, carry):
            to = lax.rem(r + step, 16)
            send(pay.at[g, to], got_a.at[g, step - 1],
                 ar_send.at[g, 0], ar_recv.at[g, 0], (to, c))
            return carry

        lax.fori_loop(1, 16, one, 0)

    def reduce_sibling(g):
        wait(got_a.at[g], ar_recv.at[g, 0])
        red_a[g] = pay[g, r] + jnp.sum(got_a[g], axis=0)
        send(red_a.at[g], got_s.at[g], ar_send.at[g, 1], ar_recv.at[g, 1], (r, sib))

    def reduce_z(g):
        wait(got_s.at[g], ar_recv.at[g, 1])
        red_b[g] = red_a[g] + got_s[g]

        def one(step, carry):
            send(red_b.at[g], got_b.at[g, step - 1],
                 ar_send.at[g, 2], ar_recv.at[g, 2], along_z(step))
            return carry

        lax.fori_loop(1, 8, one, 0)

    def reduce_share(g):
        wait(got_b.at[g], ar_recv.at[g, 2])
        got_c[g, r] = red_b[g] + jnp.sum(got_b[g], axis=0)

        def one(step, carry):
            mine_now = got_c.at[g, r]
            send(mine_now, mine_now, ar_send.at[g, 3], ar_recv.at[g, 3],
                 (lax.rem(r + step, 16), c))
            return carry

        lax.fori_loop(1, 16, one, 0)

    def reduce_end(g):
        wait(got_c.at[g, pl.ds(0, 15)], ar_recv.at[g, 3])
        xs = got_c[g, :, pl.ds(0, 8), :].reshape(T, T)
        xd = got_c[g, :, pl.ds(8, 8), :].reshape(T, T)
        dd = got_c[g, :, pl.ds(16, 8), :].reshape(T, T)
        h = (xs + xd) * (1.0 / VERTS) - eye
        terms = dd - 2.0 * (h * xd) + h * mm(xs, h)
        colsq = jnp.maximum(jnp.sum(terms, axis=0, keepdims=True), 0.0)
        scale = lax.rsqrt(colsq * (1.0 / VERTS) + 1e-06)
        return h, jnp.sum(eye * scale, axis=1, keepdims=True)

    def squares(value):
        square = value * value
        return square[:T] + square[T:]

    def order_slots():
        slots = lax.broadcasted_iota(jnp.int32, (1, T), 1)
        alive = slots < live_ref[0, 0]
        row = jnp.where(alive, rows_ref[...], 32)
        key = row * T + slots

        def column(value):
            spread = jnp.where(lane == sub, jnp.broadcast_to(value, (T, T)), 0)
            return jnp.sum(spread, axis=1, keepdims=True)

        def count(mask, axis):
            return jnp.sum(mask.astype(jnp.int32), axis=axis, keepdims=True)

        row_c, key_c, col_c = column(row), column(key), column(cols_ref[...])
        rank = count(jnp.broadcast_to(key, (T, T)) < key_c, 1)
        below = count(jnp.broadcast_to(row, (T, T)) < row_c, 1)
        here = (rank == lane).astype(jnp.int32)
        place = (col_c // 2 % 2) * 16 + (col_c // 4) * 2 + col_c % 2
        slot_of = jnp.sum(here * sub, axis=0, keepdims=True)
        place_of = jnp.sum(here * place, axis=0, keepdims=True)
        first_of = jnp.sum(here * below, axis=0, keepdims=True) == slots
        upto = count(row_c <= lane, 0)
        same = count(row_c == lane, 0)
        index_v[0:1, :] = jnp.minimum(slot_of, SLOTS - 1)
        index_v[1:2, :] = place_of
        index_v[2:3, :] = first_of.astype(jnp.int32)
        index_v[3:4, :] = jnp.where(same > 0, upto - 1, SLOTS)
        copy = pltpu.make_async_copy(index_v, index_s, index_sem)
        copy.start()
        copy.wait()

    x0 = x_ref[...]
    put_block(0, x0)
    pl.semaphore_wait(barrier, 23)

    gather_start(0)
    order_slots()
    running[SLOTS] = jnp.zeros((T, T), F32)
    gather_middle(0)
    pay[0, :, pl.ds(0, 8), :] = gram_of(x_ref[...], x_ref[...]).reshape(16, 8, T)
    tile_copy.wait()
    gather_end(0)
    products(0)
    scatter_start(0)
    scatter_middle(0)
    d0_ref[...] = scatter_end(0)

    put_block(1, d0_ref[...])
    gather_start(1)
    d0 = d0_ref[...]
    reduce_start(0, gram_of(x_ref[...], d0), squares(d0))
    gather_middle(1)
    reduce_sibling(0)
    gather_end(1)
    reduce_z(0)
    products(1)
    reduce_share(0)
    scatter_start(1)
    scatter_middle(1)
    h0, n0 = reduce_end(0)
    g1 = n0 * rot1_ref[pl.ds(T, T), :]
    h0g1 = mm(h0, g1)
    g2 = rot1_ref[pl.ds(0, T), :] - h0g1
    p1_ref[...] = mm(d0_ref[...], g1) - mm(x_ref[...], h0g1)
    x1_ref[...] = mm(x_ref[...], rot1_ref[pl.ds(0, T), :]) + p1_ref[...]
    dp1_ref[...] = -mm(d0_ref[...], h0g1)
    d1_ref[...] = mm(d0_ref[...], rot1_ref[pl.ds(0, T), :])
    u0g1 = mm(scatter_end(1), g1)
    dp1 = dp1_ref[...] + u0g1
    d1 = d1_ref[...] + dp1
    put_block(2, d1)

    gather_start(2)
    dp1_ref[...] = dp1
    d1_ref[...] = d1
    x1 = x1_ref[...]
    pay[1, :, pl.ds(0, 8), :] = gram_of(x1, x1).reshape(16, 8, T)
    reduce_start(1, gram_of(x1, d1_ref[...]), squares(d1_ref[...]))
    gather_middle(2)
    reduce_sibling(1)
    gather_end(2)
    reduce_z(1)
    products(2)
    reduce_share(1)
    scatter_start(2)
    scatter_middle(2)
    h1, n1 = reduce_end(1)
    q1 = n1 * rot2_ref[pl.ds(T, T), :]
    q2 = rot2_ref[pl.ds(0, T), :] - mm(h1, q1)
    qp = rot2_ref[pl.ds(2 * T, T), :]
    block = mm(x1_ref[...], q2) + mm(d1_ref[...], q1) + mm(p1_ref[...], qp)
    block_ref[...] = block
    image_ref[...] = mm(d1_ref[...], q2) + mm(dp1_ref[...], qp)
    image_ref[...] += block_ref[...] + mm(scatter_end(2), q1)

    for op in range(OPS):
        wait(panels[op].at[pl.ds(0, 30)], ag_send.at[op])
        wait(panels[op].at[pl.ds(0, 24)], rs_send.at[op, 0])
        wait(panels[op].at[pl.ds(0, 6)], rs_send.at[op, 1])
    for g in range(2):
        wait(got_a.at[g], ar_send.at[g, 0])
        wait(got_s.at[g], ar_send.at[g, 1])
        wait(got_b.at[g], ar_send.at[g, 2])
        wait(got_c.at[g, pl.ds(0, 15)], ar_send.at[g, 3])


def local(
    start_block, vertex_scale, adj_tiles, tile_row, tile_col, live_count,
    rotation_first, rotation_second,
):
    pad = ((0, 0), (0, T - SLOTS))
    vmem = pl.BlockSpec(memory_space=pltpu.VMEM)
    tile = (T, T)
    out = jax.ShapeDtypeStruct((2 * T, T), F32)
    dma = pltpu.SemaphoreType.DMA
    return pl.pallas_call(
        kernel,
        out_shape=(out, out),
        in_specs=[
            vmem, vmem, pl.BlockSpec(memory_space=pl.ANY), vmem, vmem,
            pl.BlockSpec(memory_space=pltpu.SMEM), vmem, vmem,
        ],
        out_specs=(vmem, vmem),
        scratch_shapes=[
            pltpu.VMEM((SLOTS, *tile), BF16),
            pltpu.VMEM((32, *tile), BF16),
            pltpu.VMEM((32, *tile), BF16),
            pltpu.VMEM((32, *tile), BF16),
            pltpu.VMEM((SLOTS + 1, *tile), F32),
            pltpu.VMEM((8, T), jnp.int32),
            pltpu.SMEM((8, T), jnp.int32),
        ]
        + [pltpu.VMEM((2 * T, T), F32)] * 7
        + [
            pltpu.VMEM((OPS, 4, 4, *tile), BF16),
            pltpu.VMEM((OPS, 4, 4, *tile), BF16),
            pltpu.VMEM((OPS, 3, 4, *tile), BF16),
            pltpu.VMEM((OPS, 3, 4, *tile), BF16),
        ]
        + [pltpu.VMEM((OPS, 3, *tile), BF16)] * 4
        + [
            pltpu.VMEM((2, 16, 24, T), F32),
            pltpu.VMEM((2, 24, T), F32),
            pltpu.VMEM((2, 15, 24, T), F32),
            pltpu.VMEM((2, 24, T), F32),
            pltpu.VMEM((2, 24, T), F32),
            pltpu.VMEM((2, 7, 24, T), F32),
            pltpu.VMEM((2, 16, 24, T), F32),
            dma,
            dma,
            dma((OPS,)),
            dma((OPS, 9)),
            dma((OPS, 2)),
            dma((OPS, 4)),
            dma((2, 4)),
            dma((2, 4)),
        ],
        compiler_params=pltpu.CompilerParams(
            collective_id=0, has_side_effects=True, vmem_limit_bytes=48 << 20
        ),
        name="lobpcg",
    )(
        start_block,
        vertex_scale.reshape(2, T),
        adj_tiles[0, 0],
        jnp.pad(tile_row[0], pad),
        jnp.pad(tile_col[0], pad),
        live_count,
        rotation_first,
        rotation_second,
    )


def solution(mesh):
    placed = (
        P(("row", "col"), None),
        P(("row", "col")),
        P("row", "col", None, None, None),
        P("row", "col", None),
        P("row", "col", None),
        P("row", "col"),
        P(),
        P(),
    )
    return jax.shard_map(
        local,
        mesh=mesh,
        in_specs=placed,
        out_specs=(P(("row", "col"), None), P(("row", "col"), None)),
        check_vma=False,
    )
```

time: 1110 us -> 106 us (0.10)
  waiting for transfers between devices: 813 us -> 0 us
  blocking collectives: 149 us -> 0 us
  Pallas kernels: 0 us -> 96.4 us
  other arithmetic: 46.7 us -> 0 us
  local copies, waits for them, and re-layouts: 52.7 us -> 7.64 us
  matrix products: 22.4 us -> 0 us
  between operations: 15.4 us -> 1.29 us
    psum x2 -> x0, waiting for transfers between devices: 485 us -> none  [residual_block(): gram = lax.psum(inner(block, image), ('row', 'col')) / verts_all]
    reduce_scatter x3 -> x0, waiting for transfers between devices: 222 us -> none  [apply_operator(): lax.psum_scatter(partial_value.astype(jnp.bfloat16), 'row', scatter_dimen...]
    psum x2 -> x0, blocking collectives: 149 us -> none  [residual_block(): colsq = lax.psum(jnp.sum(resid * resid, axis=0), ('row', 'col'))]
    all_gather x3 -> x0, waiting for transfers between devices: 105 us -> none  [apply_operator(): gathered = lax.all_gather(scaled, 'col', axis=0, tiled=True)]
    pallas_call x0 -> x1, Pallas kernels: none -> 96.4 us  [local(): pl.pallas_call(kernel, out_shape=(out, out), in_specs=[vmem, vmem, pl.Blo...]
    scatter-add x3 -> x0, other arithmetic: 31.9 us -> none  [place_rows(): placed = jax.ops.segment_sum(tile_out, rows_slot, num_segments=row_tiles)]
    dot_general x17 -> x0, matrix products: 22.4 us -> none  [the longest x3 10.8 us: tile_products(): jnp.einsum('tab,tbk->tak', tiles_here, pieces, preferred_element_type=jnp...]
    dot_general x4 -> x0, local copies, waits for them, and re-layouts: 16.9 us -> none  [the longest x3 16.8 us: tile_products(): jnp.einsum('tab,tbk->tak', tiles_here, pieces, preferred_element_type=jnp...]
  transfers between devices with their start and end apart: 8 -> 0, of which waited for: 8 -> 0; matrix products, arithmetic and copies ran while one was open for 0% -> 0% of each run, Pallas kernels for 0% -> 0%
where the time goes in v1:
time: 106 us; the launch traced here: 105 us
  Pallas kernels  96.4 us (91%)
  local copies, waits for them, and re-layouts  7.64 us (7%)
  between operations  1.29 us (1%)
    pallas_call x1, Pallas kernels, local(): pl.pallas_call(kernel, out_shape=(out, out), in_specs=[vmem, vmem, pl.Blo...  96.4 us
    unnamed x12, local copies, waits for them, and re-layouts  6.32 us

profile of v1, /device:TPU:1, one launch (start us, length us, event | category | flops | bytes accessed | tf_op | source)
XLA Modules:
  0.0 105.3 jit_solution(393520996976613267)
XLA Ops:
  1.3 0.7 pad.7.rows_ref
  1.9 0.7 pad.8.cols_ref
  2.6 0.0 copy-start
  2.6 1.6 %copy-done = bf16[1,1,64,128,128]{4,3,2,1,0:T(8,128)(2,1)S(1)} copy-done((bf16[1,1,64,128,128]{4,3,2,1,0:T(8,128)(2,1)S(1)}, bf16[1,1,64,128,128]{4,3,2,1,0:T(8,128)(2,1)}, u32[]{:S(2)}) %copy-start) | copy-done | bytes 2097176
  4.2 0.0 copy-start.1
  4.2 0.9 copy-done.1
  5.1 0.0 copy-start.2
  5.1 0.9 copy-done.2
  6.0 0.0 copy-start.3
  6.0 0.9 copy-done.3
  6.9 0.0 copy-start.4
  6.9 0.7 copy-done.4
  7.6 96.4 %lobpcg.1 = (f32[256,128]{1,0:T(8,128)S(1)}, f32[256,128]{1,0:T(8,128)S(1)}) custom-call(f32[256,128]{1,0:T(8,128)S(1)} %copy-done.2, f32[2,128]{1,0:T(2,128)S(1)} %bitcast.5, bf16[64,128,128]{2,1,0:T(8,128)(2,1)S(1)} %bitcast.4, s32[1,128]{1,0:T(1,128)S(1)} %pad.7.rows_ref, s32[1,128]{1,0:T(1,128)S(1)} %pad.8.cols_ref, s32[1,1]{1,0:T(1,128)S(6)} %copy.12.live_ref, ...), custom_call_target="tpu_custom_call" | custom-call | tf_op jit(solution)/shard_map/lobpcg/pallas_call | solution.py:365
  104.0 0.7 copy.13
  104.7 0.7 copy.14
Async XLA Ops:
  2.6 1.6 %copy-start = (bf16[1,1,64,128,128]{4,3,2,1,0:T(8,128)(2,1)S(1)}, bf16[1,1,64,128,128]{4,3,2,1,0:T(8,128)(2,1)}, u32[]{:S(2)}) copy-start(bf16[1,1,64,128,128]{4,3,2,1,0:T(8,128)(2,1)} %param.10) | copy-start | bytes 6291460
  4.2 0.9 copy-start.1
  5.1 0.9 copy-start.2
  6.0 0.9 copy-start.3
  6.9 0.7 copy-start.4

commit v2 on v1

--- a/solution.py
+++ b/solution.py
@@ -26,12 +26,13 @@
 
 
 def kernel(
-    x_ref, scale_ref, tiles_hbm, rows_ref, cols_ref, live_ref, rot1_ref, rot2_ref,
+    x_hbm, scale_hbm, tiles_hbm, rows_hbm, cols_hbm, live_hbm, rot1_hbm, rot2_hbm,
     block_ref, image_ref,
-    tiles, panel_0, panel_1, panel_2, running, index_v, index_s, s_b, d0_ref, x1_ref, d1_ref, p1_ref, dp1_ref, part,
+    x_ref, scale_ref, rows_ref, cols_ref, live_ref, rot1_ref, rot2_ref,
+    tiles, panel_0, panel_1, panel_2, running, index_v, index_s, s_b, d0_ref, u0_ref, g1_ref, g2_ref, x1_ref, d1_ref, p1_ref, dp1_ref, part,
     send_x, send_y, recv_x, recv_y, mid_x, mid_y, last_x, last_y,
     pay, red_a, got_a, red_b, got_s, got_b, got_c,
-    tile_sem, index_sem, ag_send, ag_recv, rs_send, rs_recv, ar_send, ar_recv,
+    in_sem, index_sem, ag_send, ag_recv, rs_send, rs_recv, ar_send, ar_recv,
 ):
     panels = (panel_0, panel_1, panel_2)
     r = lax.axis_index("row")
@@ -58,8 +59,15 @@
     def wait(ref, sem):
         pltpu.make_async_copy(ref, ref, sem).wait()
 
-    tile_copy = pltpu.make_async_copy(tiles_hbm, tiles, tile_sem)
-    tile_copy.start()
+    loads = [
+        pltpu.make_async_copy(source, target, in_sem.at[at])
+        for at, (source, target) in enumerate((
+            (x_hbm, x_ref), (scale_hbm, scale_ref), (rows_hbm, rows_ref), (cols_hbm, cols_ref),
+            (tiles_hbm, tiles), (rot1_hbm, rot1_ref), (rot2_hbm, rot2_ref), (live_hbm, live_ref),
+        ))
+    ]
+    for load in loads:
+        load.start()
 
     barrier = pltpu.get_barrier_semaphore()
 
@@ -80,6 +88,7 @@
     lane = lax.broadcasted_iota(jnp.int32, (T, T), 1)
     sub = lax.broadcasted_iota(jnp.int32, (T, T), 0)
     eye = (lane == sub).astype(F32)
+    loads[1].wait()
     for half in range(2):
         column = jnp.sum(eye * scale_ref[pl.ds(half, 1), :], axis=1, keepdims=True)
         s_b[pl.ds(half * T, T), :] = jnp.broadcast_to(column, (T, T))
@@ -248,46 +257,52 @@
         return square[:T] + square[T:]
 
     def order_slots():
-        slots = lax.broadcasted_iota(jnp.int32, (1, T), 1)
-        alive = slots < live_ref[0, 0]
-        row = jnp.where(alive, rows_ref[...], 32)
-        key = row * T + slots
+        wide = (SLOTS, SLOTS)
+        slots = lax.broadcasted_iota(jnp.int32, (1, SLOTS), 1)
+        at_lane = lax.broadcasted_iota(jnp.int32, wide, 1)
+        at_sub = lax.broadcasted_iota(jnp.int32, wide, 0)
+        row = jnp.where(slots < live_ref[0, 0], rows_ref[...], 32)
+        key = row * SLOTS + slots
 
         def column(value):
-            spread = jnp.where(lane == sub, jnp.broadcast_to(value, (T, T)), 0)
+            spread = jnp.where(at_lane == at_sub, jnp.broadcast_to(value, wide), 0)
             return jnp.sum(spread, axis=1, keepdims=True)
 
         def count(mask, axis):
             return jnp.sum(mask.astype(jnp.int32), axis=axis, keepdims=True)
 
         row_c, key_c, col_c = column(row), column(key), column(cols_ref[...])
-        rank = count(jnp.broadcast_to(key, (T, T)) < key_c, 1)
-        below = count(jnp.broadcast_to(row, (T, T)) < row_c, 1)
-        here = (rank == lane).astype(jnp.int32)
+        rank = count(jnp.broadcast_to(key, wide) < key_c, 1)
+        below = count(jnp.broadcast_to(row, wide) < row_c, 1)
+        here = (rank == at_lane).astype(jnp.int32)
         place = (col_c // 2 % 2) * 16 + (col_c // 4) * 2 + col_c % 2
-        slot_of = jnp.sum(here * sub, axis=0, keepdims=True)
-        place_of = jnp.sum(here * place, axis=0, keepdims=True)
         first_of = jnp.sum(here * below, axis=0, keepdims=True) == slots
-        upto = count(row_c <= lane, 0)
-        same = count(row_c == lane, 0)
-        index_v[0:1, :] = jnp.minimum(slot_of, SLOTS - 1)
-        index_v[1:2, :] = place_of
+        upto = count(row_c <= at_lane, 0)
+        same = count(row_c == at_lane, 0)
+        index_v[0:1, :] = jnp.sum(here * at_sub, axis=0, keepdims=True)
+        index_v[1:2, :] = jnp.sum(here * place, axis=0, keepdims=True)
         index_v[2:3, :] = first_of.astype(jnp.int32)
         index_v[3:4, :] = jnp.where(same > 0, upto - 1, SLOTS)
         copy = pltpu.make_async_copy(index_v, index_s, index_sem)
         copy.start()
         copy.wait()
 
+    loads[0].wait()
     x0 = x_ref[...]
     put_block(0, x0)
     pl.semaphore_wait(barrier, 23)
 
     gather_start(0)
+    loads[2].wait()
+    loads[3].wait()
+    loads[7].wait()
     order_slots()
+    loads[5].wait()
+    loads[6].wait()
     running[SLOTS] = jnp.zeros((T, T), F32)
     gather_middle(0)
     pay[0, :, pl.ds(0, 8), :] = gram_of(x_ref[...], x_ref[...]).reshape(16, 8, T)
-    tile_copy.wait()
+    loads[4].wait()
     gather_end(0)
     products(0)
     scatter_start(0)
@@ -301,46 +316,50 @@
     gather_middle(1)
     reduce_sibling(0)
     gather_end(1)
+    products(1)
+    scatter_start(1)
     reduce_z(0)
-    products(1)
+    scatter_middle(1)
     reduce_share(0)
-    scatter_start(1)
-    scatter_middle(1)
+    u0_ref[...] = scatter_end(1)
+
+    put_block(2, u0_ref[...])
+    gather_start(2)
     h0, n0 = reduce_end(0)
     g1 = n0 * rot1_ref[pl.ds(T, T), :]
     h0g1 = mm(h0, g1)
-    g2 = rot1_ref[pl.ds(0, T), :] - h0g1
-    p1_ref[...] = mm(d0_ref[...], g1) - mm(x_ref[...], h0g1)
+    g1_ref[...] = g1
+    g2_ref[...] = rot1_ref[pl.ds(0, T), :] - h0g1
+    p1_ref[...] = mm(d0_ref[...], g1)
+    p1_ref[...] -= mm(x_ref[...], h0g1)
+    dp1_ref[...] = mm(u0_ref[...], g1)
+    dp1_ref[...] -= mm(d0_ref[...], h0g1)
+    gather_middle(2)
     x1_ref[...] = mm(x_ref[...], rot1_ref[pl.ds(0, T), :]) + p1_ref[...]
-    dp1_ref[...] = -mm(d0_ref[...], h0g1)
-    d1_ref[...] = mm(d0_ref[...], rot1_ref[pl.ds(0, T), :])
-    u0g1 = mm(scatter_end(1), g1)
-    dp1 = dp1_ref[...] + u0g1
-    d1 = d1_ref[...] + dp1
-    put_block(2, d1)
-
-    gather_start(2)
-    dp1_ref[...] = dp1
-    d1_ref[...] = d1
+    d1_ref[...] = mm(d0_ref[...], rot1_ref[pl.ds(0, T), :]) + dp1_ref[...]
     x1 = x1_ref[...]
     pay[1, :, pl.ds(0, 8), :] = gram_of(x1, x1).reshape(16, 8, T)
     reduce_start(1, gram_of(x1, d1_ref[...]), squares(d1_ref[...]))
-    gather_middle(2)
+    gather_end(2)
+    products(2)
+    scatter_start(2)
     reduce_sibling(1)
-    gather_end(2)
     reduce_z(1)
-    products(2)
+    scatter_middle(2)
     reduce_share(1)
-    scatter_start(2)
-    scatter_middle(2)
+    qp = rot2_ref[pl.ds(2 * T, T), :]
+    block_ref[...] = mm(p1_ref[...], qp)
+    image_ref[...] = mm(dp1_ref[...], qp)
     h1, n1 = reduce_end(1)
     q1 = n1 * rot2_ref[pl.ds(T, T), :]
     q2 = rot2_ref[pl.ds(0, T), :] - mm(h1, q1)
-    qp = rot2_ref[pl.ds(2 * T, T), :]
-    block = mm(x1_ref[...], q2) + mm(d1_ref[...], q1) + mm(p1_ref[...], qp)
-    block_ref[...] = block
-    image_ref[...] = mm(d1_ref[...], q2) + mm(dp1_ref[...], qp)
-    image_ref[...] += block_ref[...] + mm(scatter_end(2), q1)
+    block_ref[...] += mm(d1_ref[...], q1)
+    block_ref[...] += mm(x1_ref[...], q2)
+    image_ref[...] += mm(d1_ref[...], q2)
+    image_ref[...] += mm(u0_ref[...], mm(g2_ref[...], q1))
+    image_ref[...] += block_ref[...]
+    g1q1 = mm(g1_ref[...], q1)
+    image_ref[...] += mm(scatter_end(2), g1q1)
 
     for op in range(OPS):
         wait(panels[op].at[pl.ds(0, 30)], ag_send.at[op])
@@ -357,29 +376,35 @@
     start_block, vertex_scale, adj_tiles, tile_row, tile_col, live_count,
     rotation_first, rotation_second,
 ):
-    pad = ((0, 0), (0, T - SLOTS))
     vmem = pl.BlockSpec(memory_space=pltpu.VMEM)
+    hbm = pl.BlockSpec(memory_space=pl.ANY)
     tile = (T, T)
     out = jax.ShapeDtypeStruct((2 * T, T), F32)
     dma = pltpu.SemaphoreType.DMA
     return pl.pallas_call(
         kernel,
         out_shape=(out, out),
-        in_specs=[
-            vmem, vmem, pl.BlockSpec(memory_space=pl.ANY), vmem, vmem,
-            pl.BlockSpec(memory_space=pltpu.SMEM), vmem, vmem,
-        ],
+        in_specs=[hbm] * 8,
         out_specs=(vmem, vmem),
         scratch_shapes=[
+            pltpu.VMEM((2 * T, T), F32),
+            pltpu.VMEM((2, T), F32),
+            pltpu.VMEM((1, SLOTS), jnp.int32),
+            pltpu.VMEM((1, SLOTS), jnp.int32),
+            pltpu.SMEM((1, 1), jnp.int32),
+            pltpu.VMEM((2 * T, T), F32),
+            pltpu.VMEM((3 * T, T), F32),
             pltpu.VMEM((SLOTS, *tile), BF16),
             pltpu.VMEM((32, *tile), BF16),
             pltpu.VMEM((32, *tile), BF16),
             pltpu.VMEM((32, *tile), BF16),
             pltpu.VMEM((SLOTS + 1, *tile), F32),
-            pltpu.VMEM((8, T), jnp.int32),
-            pltpu.SMEM((8, T), jnp.int32),
+            pltpu.VMEM((8, SLOTS), jnp.int32),
+            pltpu.SMEM((8, SLOTS), jnp.int32),
         ]
-        + [pltpu.VMEM((2 * T, T), F32)] * 7
+        + [pltpu.VMEM((2 * T, T), F32)] * 3
+        + [pltpu.VMEM(tile, F32)] * 2
+        + [pltpu.VMEM((2 * T, T), F32)] * 5
         + [
             pltpu.VMEM((OPS, 4, 4, *tile), BF16),
             pltpu.VMEM((OPS, 4, 4, *tile), BF16),
@@ -395,7 +420,7 @@
             pltpu.VMEM((2, 24, T), F32),
             pltpu.VMEM((2, 7, 24, T), F32),
             pltpu.VMEM((2, 16, 24, T), F32),
-            dma,
+            dma((8,)),
             dma,
             dma((OPS,)),
             dma((OPS, 9)),
@@ -405,15 +430,15 @@
             dma((2, 4)),
         ],
         compiler_params=pltpu.CompilerParams(
-            collective_id=0, has_side_effects=True, vmem_limit_bytes=48 << 20
+            collective_id=0, has_side_effects=True, vmem_limit_bytes=60 << 20
         ),
         name="lobpcg",
     )(
         start_block,
         vertex_scale.reshape(2, T),
         adj_tiles[0, 0],
-        jnp.pad(tile_row[0], pad),
-        jnp.pad(tile_col[0], pad),
+        tile_row[0],
+        tile_col[0],
         live_count,
         rotation_first,
         rotation_second,

time: 106 us -> 95.5 us (0.901)
  Pallas kernels: 96.4 us -> 90.9 us
  local copies, waits for them, and re-layouts: 7.64 us -> 3.14 us
    pallas_call x1, Pallas kernels: 96.4 us -> 90.9 us  [local(): pl.pallas_call(kernel, out_shape=(out, out), in_specs=[hbm] * 8, out_spec...]
    unnamed x12 -> x2, local copies, waits for them, and re-layouts: 6.32 us -> 3.14 us
    pad x2 -> x0, local copies, waits for them, and re-layouts: 1.32 us -> none  [the longest x1 0.66 us: local(): jnp.pad(tile_row[0], pad)]
where the time goes in v2:
time: 95.5 us; the launch traced here: 95.3 us
  Pallas kernels  90.9 us (95%)
  local copies, waits for them, and re-layouts  3.14 us (3%)
  between operations  1.29 us (1%)
    pallas_call x1, Pallas kernels, local(): pl.pallas_call(kernel, out_shape=(out, out), in_specs=[hbm] * 8, out_spec...  90.9 us
    unnamed x2, local copies, waits for them, and re-layouts  3.14 us

profile of v2, /device:TPU:1, one launch (start us, length us, event | category | flops | bytes accessed | tf_op | source)
XLA Modules:
  0.0 95.3 jit_solution(310378566572058021)
XLA Ops:
  1.3 90.9 %lobpcg.1 = (f32[256,128]{1,0:T(8,128)}, f32[256,128]{1,0:T(8,128)}) custom-call(f32[256,128]{1,0:T(8,128)} %x_hbm.1, f32[2,128]{1,0:T(2,128)} %bitcast.5, bf16[64,128,128]{2,1,0:T(8,128)(2,1)} %bitcast.4, s32[1,64]{1,0:T(1,128)} %bitcast.6, s32[1,64]{1,0:T(1,128)} %bitcast.7, s32[1,1]{1,0:T(1,128)S(6)} %copy.12.live_hbm, f32[256,128]{1,0:T(8,128)} %rot1_hbm.1, ...), custom_call_target="tpu_custom_call" | custom-call | tf_op jit(solution)/shard_map/lobpcg/pallas_call | solution.py:384
  92.2 1.6 %copy.13 = f32[256,128]{1,0:T(8,128)} copy(f32[256,128]{1,0:T(8,128)} %get-tuple-element.4) | data formatting | bytes 262144
  93.8 1.6 %copy.14 = f32[256,128]{1,0:T(8,128)} copy(f32[256,128]{1,0:T(8,128)} %get-tuple-element.5) | data formatting | bytes 262144

commit v3 on v2

--- a/solution.py
+++ b/solution.py
@@ -12,7 +12,8 @@
 T = 128
 SLOTS = 64
 VERTS = 65536
-OPS = 3
+HALF = 64
+CHAINS = 6
 
 
 def mm(left, right):
@@ -29,12 +30,12 @@
     x_hbm, scale_hbm, tiles_hbm, rows_hbm, cols_hbm, live_hbm, rot1_hbm, rot2_hbm,
     block_ref, image_ref,
     x_ref, scale_ref, rows_ref, cols_ref, live_ref, rot1_ref, rot2_ref,
-    tiles, panel_0, panel_1, panel_2, running, index_v, index_s, s_b, d0_ref, u0_ref, g1_ref, g2_ref, x1_ref, d1_ref, p1_ref, dp1_ref, part,
+    tiles, panel_0, panel_1, panel_2, panel_3, panel_4, panel_5, both, running, index_v, index_s, s_b, held, d0_ref, u0_ref, g1_ref, g2_ref, x1_ref, d1_ref, p1_ref, dp1_ref, part,
     send_x, send_y, recv_x, recv_y, mid_x, mid_y, last_x, last_y,
     pay, red_a, got_a, red_b, got_s, got_b, got_c,
     in_sem, index_sem, ag_send, ag_recv, rs_send, rs_recv, ar_send, ar_recv,
 ):
-    panels = (panel_0, panel_1, panel_2)
+    panels = (panel_0, panel_1, panel_2, panel_3, panel_4, panel_5)
     r = lax.axis_index("row")
     c = lax.axis_index("col")
     x, y = r // 4, lax.rem(r, 4)
@@ -89,117 +90,152 @@
     sub = lax.broadcasted_iota(jnp.int32, (T, T), 0)
     eye = (lane == sub).astype(F32)
     loads[1].wait()
-    for half in range(2):
-        column = jnp.sum(eye * scale_ref[pl.ds(half, 1), :], axis=1, keepdims=True)
-        s_b[pl.ds(half * T, T), :] = jnp.broadcast_to(column, (T, T))
-
-    mine = (k * 8 + z) * 2
-
-    def put_block(op, value):
-        scaled = (s_b[...] * value).astype(BF16)
-        panels[op][mine] = scaled[:T]
-        panels[op][mine + 1] = scaled[T:]
+    low = lane < HALF
+
+    def turn(value):
+        return pltpu.roll(value, HALF, 1)
+
+    def scale_column(half):
+        return jnp.sum(eye * scale_ref[pl.ds(half, 1), :], axis=1, keepdims=True)
+
+    s_b[...] = jnp.where(low, scale_column(0), scale_column(1))
+
+    def pack(top, bottom):
+        return jnp.where(low, top, turn(bottom)), jnp.where(low, turn(top), bottom)
+
+    def unpack(first, second, target):
+        target[pl.ds(0, T), :] = jnp.where(low, first, turn(second))
+        target[pl.ds(T, T), :] = jnp.where(low, turn(first), second)
 
     def at_z(step):
-        return (k * 8 + lax.rem(z + step + 8, 8)) * 2
-
-    def gather_start(op):
-        own = panels[op].at[pl.ds(mine, 2)]
-        send(own, own, ag_send.at[op], ag_recv.at[op, 1], along_z(2))
-        send(own, own, ag_send.at[op], ag_recv.at[op, 2], along_z(-2))
-        send(own, own, ag_send.at[op], ag_recv.at[op, 3], along_z(1))
-        send(own, own, ag_send.at[op], ag_recv.at[op, 4], along_z(-1))
-        send(own, own, ag_send.at[op], ag_recv.at[op, 0], (r, sib))
-
-    def to_sibling(op, step):
-        block = panels[op].at[pl.ds(at_z(step), 2)]
-        send(block, block, ag_send.at[op], ag_recv.at[op, 0], (r, sib))
-
-    def gather_middle(op):
-        up = panels[op].at[pl.ds(at_z(-2), 2)]
-        low = panels[op].at[pl.ds(at_z(-2), 1)]
-        wait(up, ag_recv.at[op, 1])
-        send(low, low, ag_send.at[op], ag_recv.at[op, 5], along_z(2))
-        send(up, up, ag_send.at[op], ag_recv.at[op, 6], along_z(1))
-        down = panels[op].at[pl.ds(at_z(2), 2)]
-        high = panels[op].at[pl.ds(at_z(2) + 1, 1)]
-        wait(down, ag_recv.at[op, 2])
-        send(high, high, ag_send.at[op], ag_recv.at[op, 7], along_z(-2))
-        send(down, down, ag_send.at[op], ag_recv.at[op, 8], along_z(-1))
-        to_sibling(op, -2)
-        to_sibling(op, 2)
-        wait(panels[op].at[pl.ds(at_z(-1), 2)], ag_recv.at[op, 3])
-        to_sibling(op, -1)
-        wait(panels[op].at[pl.ds(at_z(1), 2)], ag_recv.at[op, 4])
-        to_sibling(op, 1)
-
-    def gather_end(op):
-        wait(panels[op].at[pl.ds(at_z(-3), 2)], ag_recv.at[op, 6])
-        to_sibling(op, -3)
-        wait(panels[op].at[pl.ds(at_z(3), 2)], ag_recv.at[op, 8])
-        to_sibling(op, 3)
-        wait(panels[op].at[pl.ds(at_z(4), 1)], ag_recv.at[op, 5])
-        wait(panels[op].at[pl.ds(at_z(4) + 1, 1)], ag_recv.at[op, 7])
-        to_sibling(op, 4)
-        wait(panels[op].at[pl.ds((1 - k) * 16, 16)], ag_recv.at[op, 0])
-
-    def products(op):
+        return k * 8 + lax.rem(z + step + 8, 8)
+
+    def put_block(q, value):
+        panels[q][at_z(0)] = (s_b[...] * value).astype(BF16)
+
+    def gather_start(q):
+        own = panels[q].at[at_z(0)]
+        send(own, own, ag_send.at[q], ag_recv.at[q, 1], along_z(2))
+        send(own, own, ag_send.at[q], ag_recv.at[q, 2], along_z(-2))
+        send(own, own, ag_send.at[q], ag_recv.at[q, 3], along_z(1))
+        send(own, own, ag_send.at[q], ag_recv.at[q, 4], along_z(-1))
+        send(own, own, ag_send.at[q], ag_recv.at[q, 0], (r, sib))
+
+    def to_sibling(q, step):
+        block = panels[q].at[at_z(step)]
+        send(block, block, ag_send.at[q], ag_recv.at[q, 0], (r, sib))
+
+    def gather_middle(q):
+        up = panels[q].at[at_z(-2)]
+        upper = panels[q].at[at_z(-2), pl.ds(0, HALF)]
+        wait(up, ag_recv.at[q, 1])
+        send(upper, upper, ag_send.at[q], ag_recv.at[q, 5], along_z(2))
+        send(up, up, ag_send.at[q], ag_recv.at[q, 6], along_z(1))
+        down = panels[q].at[at_z(2)]
+        lower = panels[q].at[at_z(2), pl.ds(HALF, HALF)]
+        wait(down, ag_recv.at[q, 2])
+        send(lower, lower, ag_send.at[q], ag_recv.at[q, 7], along_z(-2))
+        send(down, down, ag_send.at[q], ag_recv.at[q, 8], along_z(-1))
+        to_sibling(q, -2)
+        to_sibling(q, 2)
+        wait(panels[q].at[at_z(-1)], ag_recv.at[q, 3])
+        to_sibling(q, -1)
+        wait(panels[q].at[at_z(1)], ag_recv.at[q, 4])
+        to_sibling(q, 1)
+
+    def spread(q, core):
+        def one(at, carry):
+            block = panels[q][core * 8 + at]
+            both[core * 8 + at] = block
+            both[16 + core * 8 + at] = turn(block.astype(F32)).astype(BF16)
+            return carry
+
+        lax.fori_loop(0, 8, one, 0, unroll=8)
+
+    def gather_end(q):
+        wait(panels[q].at[at_z(-3)], ag_recv.at[q, 6])
+        to_sibling(q, -3)
+        wait(panels[q].at[at_z(3)], ag_recv.at[q, 8])
+        to_sibling(q, 3)
+        wait(panels[q].at[at_z(4), pl.ds(0, HALF)], ag_recv.at[q, 5])
+        wait(panels[q].at[at_z(4), pl.ds(HALF, HALF)], ag_recv.at[q, 7])
+        to_sibling(q, 4)
+        spread(q, k)
+        wait(panels[q].at[pl.ds((1 - k) * 8, 8)], ag_recv.at[q, 0])
+        spread(q, 1 - k)
+
+    def products(q):
         def slot(t, total):
             product = jnp.dot(
-                tiles[index_s[0, t]], panels[op][index_s[1, t]], preferred_element_type=F32
+                tiles[index_s[0, t]], both[index_s[1, t]], preferred_element_type=F32
             )
             total = jnp.where(index_s[2, t] > 0, product, total + product)
             running[t] = total
             return total
 
-        lax.fori_loop(0, SLOTS, slot, jnp.zeros((T, T), F32), unroll=8)
-
-    def scatter_start(op):
+        lax.fori_loop(0, SLOTS, slot, jnp.zeros((T, T), F32), unroll=64)
+
+    def scatter_start(q):
+        def rows(to, start):
+            return jnp.where(
+                low[:HALF],
+                running[index_s[3, to * 2], pl.ds(start, HALF)],
+                running[index_s[3, to * 2 + 1], pl.ds(start, HALF)],
+            ).astype(BF16)
+
         for step in (1, 3, 2, 0):
             for other in range(4):
-                tile = (lax.rem(x + step, 4) * 4 + other) * 2
-                send_x[op, step, other] = running[index_s[3, tile]].astype(BF16)
+                send_x[q, step, other] = rows(lax.rem(x + step, 4) * 4 + other, 0)
             if step:
-                send(send_x.at[op, step], recv_x.at[op, step - 1],
-                     rs_send.at[op, 0], rs_recv.at[op, 0], along_x(step))
+                send(send_x.at[q, step], recv_x.at[q, step - 1],
+                     rs_send.at[q, 0], rs_recv.at[q, 0], along_x(step))
             for other in range(4):
-                tile = (other * 4 + lax.rem(y + step, 4)) * 2 + 1
-                send_y[op, step, other] = running[index_s[3, tile]].astype(BF16)
+                send_y[q, step, other] = rows(other * 4 + lax.rem(y + step, 4), HALF)
             if step:
-                send(send_y.at[op, step], recv_y.at[op, step - 1],
-                     rs_send.at[op, 0], rs_recv.at[op, 1], along_y(step))
-
-    def sum_of(own, got, op, at):
+                send(send_y.at[q, step], recv_y.at[q, step - 1],
+                     rs_send.at[q, 0], rs_recv.at[q, 1], along_y(step))
+
+    def sum_of(own, got, q, at):
         return (
-            own[op, 0, at].astype(F32) + got[op, 0, at].astype(F32)
-            + got[op, 1, at].astype(F32) + got[op, 2, at].astype(F32)
+            own[q, 0, at].astype(F32) + got[q, 0, at].astype(F32)
+            + got[q, 1, at].astype(F32) + got[q, 2, at].astype(F32)
         )
 
-    def scatter_middle(op):
-        wait(recv_x.at[op], rs_recv.at[op, 0])
+    def scatter_middle(q):
+        wait(recv_x.at[q], rs_recv.at[q, 0])
         for step in (1, 3, 2):
-            mid_x[op, step - 1] = sum_of(send_x, recv_x, op, lax.rem(y + step, 4)).astype(BF16)
-            send(mid_x.at[op, step - 1], last_x.at[op, step - 1],
-                 rs_send.at[op, 1], rs_recv.at[op, 2], along_y(step))
-        wait(recv_y.at[op], rs_recv.at[op, 1])
+            mid_x[q, step - 1] = sum_of(send_x, recv_x, q, lax.rem(y + step, 4)).astype(BF16)
+            send(mid_x.at[q, step - 1], last_x.at[q, step - 1],
+                 rs_send.at[q, 1], rs_recv.at[q, 2], along_y(step))
+        wait(recv_y.at[q], rs_recv.at[q, 1])
         for step in (1, 3, 2):
-            mid_y[op, step - 1] = sum_of(send_y, recv_y, op, lax.rem(x + step, 4)).astype(BF16)
-            send(mid_y.at[op, step - 1], last_y.at[op, step - 1],
-                 rs_send.at[op, 1], rs_recv.at[op, 3], along_x(step))
-        part[pl.ds(0, T), :] = sum_of(send_x, recv_x, op, y)
-        part[pl.ds(T, T), :] = sum_of(send_y, recv_y, op, x)
-
-    def scatter_end(op):
+            mid_y[q, step - 1] = sum_of(send_y, recv_y, q, lax.rem(x + step, 4)).astype(BF16)
+            send(mid_y.at[q, step - 1], last_y.at[q, step - 1],
+                 rs_send.at[q, 1], rs_recv.at[q, 3], along_x(step))
+        part[q % 2, pl.ds(0, HALF), :] = sum_of(send_x, recv_x, q, y)
+        part[q % 2, pl.ds(HALF, HALF), :] = sum_of(send_y, recv_y, q, x)
+
+    def scatter_end(q):
         def total(last):
             return (
-                last[op, 0].astype(F32) + last[op, 1].astype(F32) + last[op, 2].astype(F32)
+                last[q, 0].astype(F32) + last[q, 1].astype(F32) + last[q, 2].astype(F32)
             )
 
-        wait(last_x.at[op], rs_recv.at[op, 2])
-        part[pl.ds(0, T), :] += total(last_x)
-        wait(last_y.at[op], rs_recv.at[op, 3])
-        part[pl.ds(T, T), :] += total(last_y)
-        return -(s_b[...] * part[...])
+        wait(last_x.at[q], rs_recv.at[q, 2])
+        part[q % 2, pl.ds(0, HALF), :] += total(last_x)
+        wait(last_y.at[q], rs_recv.at[q, 3])
+        part[q % 2, pl.ds(HALF, HALF), :] += total(last_y)
+        held[q % 2] = -(s_b[...] * part[q % 2])
+
+    def next_gather(q):
+        scatter_end(q)
+        put_block(q + 2, held[q % 2])
+        gather_start(q + 2)
+
+    def multiply(q):
+        gather_end(q)
+        products(q)
+        scatter_start(q)
 
     def reduce_start(g, xd, dd):
         pay[g, :, pl.ds(8, 8), :] = xd.reshape(16, 8, T)
@@ -275,7 +311,8 @@
         rank = count(jnp.broadcast_to(key, wide) < key_c, 1)
         below = count(jnp.broadcast_to(row, wide) < row_c, 1)
         here = (rank == at_lane).astype(jnp.int32)
-        place = (col_c // 2 % 2) * 16 + (col_c // 4) * 2 + col_c % 2
+        turned = (row_c + col_c) % 2
+        place = turned * 16 + (col_c // 2 % 2) * 8 + col_c // 4
         first_of = jnp.sum(here * below, axis=0, keepdims=True) == slots
         upto = count(row_c <= at_lane, 0)
         same = count(row_c == at_lane, 0)
@@ -288,43 +325,44 @@
         copy.wait()
 
     loads[0].wait()
-    x0 = x_ref[...]
-    put_block(0, x0)
+    for q, value in enumerate(pack(x_ref[pl.ds(0, T), :], x_ref[pl.ds(T, T), :])):
+        put_block(q, value)
     pl.semaphore_wait(barrier, 23)
 
     gather_start(0)
-    loads[2].wait()
-    loads[3].wait()
-    loads[7].wait()
+    gather_start(1)
+    for load in (2, 3, 7):
+        loads[load].wait()
     order_slots()
-    loads[5].wait()
-    loads[6].wait()
     running[SLOTS] = jnp.zeros((T, T), F32)
     gather_middle(0)
+    gather_middle(1)
     pay[0, :, pl.ds(0, 8), :] = gram_of(x_ref[...], x_ref[...]).reshape(16, 8, T)
-    loads[4].wait()
-    gather_end(0)
-    products(0)
-    scatter_start(0)
+    for load in (4, 5, 6):
+        loads[load].wait()
+    multiply(0)
+    multiply(1)
     scatter_middle(0)
-    d0_ref[...] = scatter_end(0)
-
-    put_block(1, d0_ref[...])
-    gather_start(1)
+    scatter_middle(1)
+    next_gather(0)
+    next_gather(1)
+
+    unpack(held[0], held[1], d0_ref)
     d0 = d0_ref[...]
     reduce_start(0, gram_of(x_ref[...], d0), squares(d0))
-    gather_middle(1)
+    gather_middle(2)
+    gather_middle(3)
+    multiply(2)
     reduce_sibling(0)
-    gather_end(1)
-    products(1)
-    scatter_start(1)
+    multiply(3)
     reduce_z(0)
-    scatter_middle(1)
+    scatter_middle(2)
+    scatter_middle(3)
     reduce_share(0)
-    u0_ref[...] = scatter_end(1)
-
-    put_block(2, u0_ref[...])
-    gather_start(2)
+    next_gather(2)
+    next_gather(3)
+
+    unpack(held[0], held[1], u0_ref)
     h0, n0 = reduce_end(0)
     g1 = n0 * rot1_ref[pl.ds(T, T), :]
     h0g1 = mm(h0, g1)
@@ -334,18 +372,19 @@
     p1_ref[...] -= mm(x_ref[...], h0g1)
     dp1_ref[...] = mm(u0_ref[...], g1)
     dp1_ref[...] -= mm(d0_ref[...], h0g1)
-    gather_middle(2)
+    gather_middle(4)
+    gather_middle(5)
     x1_ref[...] = mm(x_ref[...], rot1_ref[pl.ds(0, T), :]) + p1_ref[...]
     d1_ref[...] = mm(d0_ref[...], rot1_ref[pl.ds(0, T), :]) + dp1_ref[...]
     x1 = x1_ref[...]
     pay[1, :, pl.ds(0, 8), :] = gram_of(x1, x1).reshape(16, 8, T)
     reduce_start(1, gram_of(x1, d1_ref[...]), squares(d1_ref[...]))
-    gather_end(2)
-    products(2)
-    scatter_start(2)
+    multiply(4)
     reduce_sibling(1)
+    multiply(5)
     reduce_z(1)
-    scatter_middle(2)
+    scatter_middle(4)
+    scatter_middle(5)
     reduce_share(1)
     qp = rot2_ref[pl.ds(2 * T, T), :]
     block_ref[...] = mm(p1_ref[...], qp)
@@ -358,13 +397,16 @@
     image_ref[...] += mm(d1_ref[...], q2)
     image_ref[...] += mm(u0_ref[...], mm(g2_ref[...], q1))
     image_ref[...] += block_ref[...]
-    g1q1 = mm(g1_ref[...], q1)
-    image_ref[...] += mm(scatter_end(2), g1q1)
-
-    for op in range(OPS):
-        wait(panels[op].at[pl.ds(0, 30)], ag_send.at[op])
-        wait(panels[op].at[pl.ds(0, 24)], rs_send.at[op, 0])
-        wait(panels[op].at[pl.ds(0, 6)], rs_send.at[op, 1])
+    g1_ref[...] = mm(g1_ref[...], q1)
+    scatter_end(4)
+    scatter_end(5)
+    unpack(held[0], held[1], d0_ref)
+    image_ref[...] += mm(d0_ref[...], g1_ref[...])
+
+    for q in range(CHAINS):
+        wait(both.at[pl.ds(0, 15)], ag_send.at[q])
+        wait(both.at[pl.ds(0, 12)], rs_send.at[q, 0])
+        wait(both.at[pl.ds(0, 3)], rs_send.at[q, 1])
     for g in range(2):
         wait(got_a.at[g], ar_send.at[g, 0])
         wait(got_s.at[g], ar_send.at[g, 1])
@@ -395,23 +437,22 @@
             pltpu.VMEM((2 * T, T), F32),
             pltpu.VMEM((3 * T, T), F32),
             pltpu.VMEM((SLOTS, *tile), BF16),
-            pltpu.VMEM((32, *tile), BF16),
-            pltpu.VMEM((32, *tile), BF16),
+        ]
+        + [pltpu.VMEM((16, *tile), BF16)] * CHAINS
+        + [
             pltpu.VMEM((32, *tile), BF16),
             pltpu.VMEM((SLOTS + 1, *tile), F32),
             pltpu.VMEM((8, SLOTS), jnp.int32),
             pltpu.SMEM((8, SLOTS), jnp.int32),
         ]
-        + [pltpu.VMEM((2 * T, T), F32)] * 3
+        + [pltpu.VMEM(tile, F32), pltpu.VMEM((2, *tile), F32)]
+        + [pltpu.VMEM((2 * T, T), F32)] * 2
         + [pltpu.VMEM(tile, F32)] * 2
-        + [pltpu.VMEM((2 * T, T), F32)] * 5
-        + [
-            pltpu.VMEM((OPS, 4, 4, *tile), BF16),
-            pltpu.VMEM((OPS, 4, 4, *tile), BF16),
-            pltpu.VMEM((OPS, 3, 4, *tile), BF16),
-            pltpu.VMEM((OPS, 3, 4, *tile), BF16),
-        ]
-        + [pltpu.VMEM((OPS, 3, *tile), BF16)] * 4
+        + [pltpu.VMEM((2 * T, T), F32)] * 4
+        + [pltpu.VMEM((2, *tile), F32)]
+        + [pltpu.VMEM((CHAINS, 4, 4, HALF, T), BF16)] * 2
+        + [pltpu.VMEM((CHAINS, 3, 4, HALF, T), BF16)] * 2
+        + [pltpu.VMEM((CHAINS, 3, HALF, T), BF16)] * 4
         + [
             pltpu.VMEM((2, 16, 24, T), F32),
             pltpu.VMEM((2, 24, T), F32),
@@ -422,10 +463,10 @@
             pltpu.VMEM((2, 16, 24, T), F32),
             dma((8,)),
             dma,
-            dma((OPS,)),
-            dma((OPS, 9)),
-            dma((OPS, 2)),
-            dma((OPS, 4)),
+            dma((CHAINS,)),
+            dma((CHAINS, 9)),
+            dma((CHAINS, 2)),
+            dma((CHAINS, 4)),
             dma((2, 4)),
             dma((2, 4)),
         ],

time: 95.5 us -> 86.6 us (0.907)
  Pallas kernels: 90.9 us -> 82.1 us
    pallas_call x1, Pallas kernels: 90.9 us -> 82.1 us  [local(): pl.pallas_call(kernel, out_shape=(out, out), in_specs=[hbm] * 8, out_spec...]
where the time goes in v3:
time: 86.6 us; the launch traced here: 86.5 us
  Pallas kernels  82.1 us (95%)
  local copies, waits for them, and re-layouts  3.14 us (4%)
  between operations  1.29 us (1%)
    pallas_call x1, Pallas kernels, local(): pl.pallas_call(kernel, out_shape=(out, out), in_specs=[hbm] * 8, out_spec...  82.1 us
    unnamed x2, local copies, waits for them, and re-layouts  3.14 us

profile of v3, /device:TPU:1, one launch (start us, length us, event | category | flops | bytes accessed | tf_op | source)
XLA Modules:
  0.0 86.5 jit_solution(555641493261330228)
XLA Ops:
  1.3 82.1 %lobpcg.1 = (f32[256,128]{1,0:T(8,128)}, f32[256,128]{1,0:T(8,128)}) custom-call(f32[256,128]{1,0:T(8,128)} %x_hbm.1, f32[2,128]{1,0:T(2,128)} %bitcast.5, bf16[64,128,128]{2,1,0:T(8,128)(2,1)} %bitcast.4, s32[1,64]{1,0:T(1,128)} %bitcast.6, s32[1,64]{1,0:T(1,128)} %bitcast.7, s32[1,1]{1,0:T(1,128)S(6)} %copy.12.live_hbm, f32[256,128]{1,0:T(8,128)} %rot1_hbm.1, ...), custom_call_target="tpu_custom_call" | custom-call | tf_op jit(solution)/shard_map/lobpcg/pallas_call | solution.py:426
  83.3 1.6 %copy.13 = f32[256,128]{1,0:T(8,128)} copy(f32[256,128]{1,0:T(8,128)} %get-tuple-element.4) | data formatting | bytes 262144
  84.9 1.6 %copy.14 = f32[256,128]{1,0:T(8,128)} copy(f32[256,128]{1,0:T(8,128)} %get-tuple-element.5) | data formatting | bytes 262144

commit v4 on v3

--- a/solution.py
+++ b/solution.py
@@ -13,6 +13,7 @@
 SLOTS = 64
 VERTS = 65536
 HALF = 64
+ROWS = 17
 CHAINS = 6
 
 
@@ -30,7 +31,7 @@
     x_hbm, scale_hbm, tiles_hbm, rows_hbm, cols_hbm, live_hbm, rot1_hbm, rot2_hbm,
     block_ref, image_ref,
     x_ref, scale_ref, rows_ref, cols_ref, live_ref, rot1_ref, rot2_ref,
-    tiles, panel_0, panel_1, panel_2, panel_3, panel_4, panel_5, both, running, index_v, index_s, s_b, held, d0_ref, u0_ref, g1_ref, g2_ref, x1_ref, d1_ref, p1_ref, dp1_ref, part,
+    tiles, panel_0, panel_1, panel_2, panel_3, panel_4, panel_5, both, running, index_v, index_s, s_b, held, basis, next_ref, last_ref, g_ref, q_ref, part,
     send_x, send_y, recv_x, recv_y, mid_x, mid_y, last_x, last_y,
     pay, red_a, got_a, red_b, got_s, got_b, got_c,
     in_sem, index_sem, ag_send, ag_recv, rs_send, rs_recv, ar_send, ar_recv,
@@ -103,9 +104,10 @@
     def pack(top, bottom):
         return jnp.where(low, top, turn(bottom)), jnp.where(low, turn(top), bottom)
 
-    def unpack(first, second, target):
-        target[pl.ds(0, T), :] = jnp.where(low, first, turn(second))
-        target[pl.ds(T, T), :] = jnp.where(low, turn(first), second)
+    def unpack(target, at):
+        first, second = held[0], held[1]
+        target[pl.ds(0, T), pl.ds(at, T)] = jnp.where(low, first, turn(second))
+        target[pl.ds(T, T), pl.ds(at, T)] = jnp.where(low, turn(first), second)
 
     def at_z(step):
         return k * 8 + lax.rem(z + step + 8, 8)
@@ -233,13 +235,12 @@
         gather_start(q + 2)
 
     def multiply(q):
-        gather_end(q)
         products(q)
         scatter_start(q)
 
     def reduce_start(g, xd, dd):
         pay[g, :, pl.ds(8, 8), :] = xd.reshape(16, 8, T)
-        pay[g, :, pl.ds(16, 8), :] = dd.reshape(16, 8, T)
+        pay[g, :, 16, :] = dd
 
         def one(step, carry):
             to = lax.rem(r + step, 16)
@@ -281,16 +282,15 @@
         wait(got_c.at[g, pl.ds(0, 15)], ar_recv.at[g, 3])
         xs = got_c[g, :, pl.ds(0, 8), :].reshape(T, T)
         xd = got_c[g, :, pl.ds(8, 8), :].reshape(T, T)
-        dd = got_c[g, :, pl.ds(16, 8), :].reshape(T, T)
+        dd = jnp.sum(got_c[g, :, 16, :], axis=0, keepdims=True)
         h = (xs + xd) * (1.0 / VERTS) - eye
-        terms = dd - 2.0 * (h * xd) + h * mm(xs, h)
-        colsq = jnp.maximum(jnp.sum(terms, axis=0, keepdims=True), 0.0)
+        terms = h * mm(xs, h) - 2.0 * (h * xd)
+        colsq = jnp.maximum(dd + jnp.sum(terms, axis=0, keepdims=True), 0.0)
         scale = lax.rsqrt(colsq * (1.0 / VERTS) + 1e-06)
         return h, jnp.sum(eye * scale, axis=1, keepdims=True)
 
     def squares(value):
-        square = value * value
-        return square[:T] + square[T:]
+        return jnp.sum((value * value).reshape(16, 16, T), axis=0)
 
     def order_slots():
         wide = (SLOTS, SLOTS)
@@ -335,73 +335,80 @@
         loads[load].wait()
     order_slots()
     running[SLOTS] = jnp.zeros((T, T), F32)
+    basis[:, pl.ds(0, T)] = x_ref[...]
     gather_middle(0)
     gather_middle(1)
     pay[0, :, pl.ds(0, 8), :] = gram_of(x_ref[...], x_ref[...]).reshape(16, 8, T)
     for load in (4, 5, 6):
         loads[load].wait()
+    gather_end(0)
     multiply(0)
+    gather_end(1)
     multiply(1)
     scatter_middle(0)
     scatter_middle(1)
     next_gather(0)
     next_gather(1)
 
-    unpack(held[0], held[1], d0_ref)
-    d0 = d0_ref[...]
+    unpack(basis, T)
+    d0 = basis[:, pl.ds(T, T)]
     reduce_start(0, gram_of(x_ref[...], d0), squares(d0))
     gather_middle(2)
     gather_middle(3)
+    reduce_sibling(0)
+    gather_end(2)
     multiply(2)
-    reduce_sibling(0)
+    reduce_z(0)
+    gather_end(3)
     multiply(3)
-    reduce_z(0)
     scatter_middle(2)
+    reduce_share(0)
     scatter_middle(3)
-    reduce_share(0)
     next_gather(2)
     next_gather(3)
 
-    unpack(held[0], held[1], u0_ref)
+    unpack(basis, 2 * T)
     h0, n0 = reduce_end(0)
     g1 = n0 * rot1_ref[pl.ds(T, T), :]
     h0g1 = mm(h0, g1)
-    g1_ref[...] = g1
-    g2_ref[...] = rot1_ref[pl.ds(0, T), :] - h0g1
-    p1_ref[...] = mm(d0_ref[...], g1)
-    p1_ref[...] -= mm(x_ref[...], h0g1)
-    dp1_ref[...] = mm(u0_ref[...], g1)
-    dp1_ref[...] -= mm(d0_ref[...], h0g1)
+    g_ref[pl.ds(0, T), :] = rot1_ref[pl.ds(0, T), :] - h0g1
+    g_ref[pl.ds(T, T), :] = g1
+    next_ref[:, pl.ds(0, T)] = mm(basis[:, pl.ds(0, 2 * T)], g_ref[...])
+    next_ref[:, pl.ds(T, T)] = mm(basis[:, pl.ds(T, 2 * T)], g_ref[...])
     gather_middle(4)
     gather_middle(5)
-    x1_ref[...] = mm(x_ref[...], rot1_ref[pl.ds(0, T), :]) + p1_ref[...]
-    d1_ref[...] = mm(d0_ref[...], rot1_ref[pl.ds(0, T), :]) + dp1_ref[...]
-    x1 = x1_ref[...]
+    x1 = next_ref[:, pl.ds(0, T)]
+    d1 = next_ref[:, pl.ds(T, T)]
     pay[1, :, pl.ds(0, 8), :] = gram_of(x1, x1).reshape(16, 8, T)
-    reduce_start(1, gram_of(x1, d1_ref[...]), squares(d1_ref[...]))
+    reduce_start(1, gram_of(x1, d1), squares(d1))
+    gather_end(4)
+    reduce_sibling(1)
     multiply(4)
-    reduce_sibling(1)
+    reduce_z(1)
+    gather_end(5)
     multiply(5)
-    reduce_z(1)
+    qp = rot2_ref[pl.ds(2 * T, T), :]
+    q_ref[pl.ds(T, T), :] = mm(g_ref[pl.ds(T, T), :], qp)
+    q_ref[pl.ds(0, T), :] = mm(g_ref[pl.ds(0, T), :] - rot1_ref[pl.ds(0, T), :], qp)
+    block_ref[...] = mm(basis[:, pl.ds(0, 2 * T)], q_ref[...])
+    image_ref[...] = mm(basis[:, pl.ds(T, 2 * T)], q_ref[...])
     scatter_middle(4)
+    reduce_share(1)
     scatter_middle(5)
-    reduce_share(1)
-    qp = rot2_ref[pl.ds(2 * T, T), :]
-    block_ref[...] = mm(p1_ref[...], qp)
-    image_ref[...] = mm(dp1_ref[...], qp)
     h1, n1 = reduce_end(1)
     q1 = n1 * rot2_ref[pl.ds(T, T), :]
-    q2 = rot2_ref[pl.ds(0, T), :] - mm(h1, q1)
-    block_ref[...] += mm(d1_ref[...], q1)
-    block_ref[...] += mm(x1_ref[...], q2)
-    image_ref[...] += mm(d1_ref[...], q2)
-    image_ref[...] += mm(u0_ref[...], mm(g2_ref[...], q1))
+    q_ref[pl.ds(0, T), :] = rot2_ref[pl.ds(0, T), :] - mm(h1, q1)
+    q_ref[pl.ds(T, T), :] = q1
+    block_ref[...] += mm(next_ref[...], q_ref[...])
+    image_ref[...] += mm(next_ref[:, pl.ds(T, T)], q_ref[pl.ds(0, T), :])
+    q_ref[pl.ds(0, T), :] = mm(g_ref[pl.ds(0, T), :], q1)
+    q_ref[pl.ds(T, T), :] = mm(g_ref[pl.ds(T, T), :], q1)
+    image_ref[...] += mm(basis[:, pl.ds(2 * T, T)], q_ref[pl.ds(0, T), :])
     image_ref[...] += block_ref[...]
-    g1_ref[...] = mm(g1_ref[...], q1)
     scatter_end(4)
     scatter_end(5)
-    unpack(held[0], held[1], d0_ref)
-    image_ref[...] += mm(d0_ref[...], g1_ref[...])
+    unpack(last_ref, 0)
+    image_ref[...] += mm(last_ref[...], q_ref[pl.ds(T, T), :])
 
     for q in range(CHAINS):
         wait(both.at[pl.ds(0, 15)], ag_send.at[q])
@@ -446,21 +453,20 @@
             pltpu.SMEM((8, SLOTS), jnp.int32),
         ]
         + [pltpu.VMEM(tile, F32), pltpu.VMEM((2, *tile), F32)]
-        + [pltpu.VMEM((2 * T, T), F32)] * 2
-        + [pltpu.VMEM(tile, F32)] * 2
-        + [pltpu.VMEM((2 * T, T), F32)] * 4
+        + [pltpu.VMEM((2 * T, 3 * T), F32), pltpu.VMEM((2 * T, 2 * T), F32)]
+        + [pltpu.VMEM((2 * T, T), F32)] * 3
         + [pltpu.VMEM((2, *tile), F32)]
         + [pltpu.VMEM((CHAINS, 4, 4, HALF, T), BF16)] * 2
         + [pltpu.VMEM((CHAINS, 3, 4, HALF, T), BF16)] * 2
         + [pltpu.VMEM((CHAINS, 3, HALF, T), BF16)] * 4
         + [
-            pltpu.VMEM((2, 16, 24, T), F32),
-            pltpu.VMEM((2, 24, T), F32),
-            pltpu.VMEM((2, 15, 24, T), F32),
-            pltpu.VMEM((2, 24, T), F32),
-            pltpu.VMEM((2, 24, T), F32),
-            pltpu.VMEM((2, 7, 24, T), F32),
-            pltpu.VMEM((2, 16, 24, T), F32),
+            pltpu.VMEM((2, 16, ROWS, T), F32),
+            pltpu.VMEM((2, ROWS, T), F32),
+            pltpu.VMEM((2, 15, ROWS, T), F32),
+            pltpu.VMEM((2, ROWS, T), F32),
+            pltpu.VMEM((2, ROWS, T), F32),
+            pltpu.VMEM((2, 7, ROWS, T), F32),
+            pltpu.VMEM((2, 16, ROWS, T), F32),
             dma((8,)),
             dma,
             dma((CHAINS,)),

time: 86.6 us -> 83.5 us (0.964)
  Pallas kernels: 82.1 us -> 78.9 us
    pallas_call x1, Pallas kernels: 82.1 us -> 78.9 us  [local(): pl.pallas_call(kernel, out_shape=(out, out), in_specs=[hbm] * 8, out_spec...]
where the time goes in v4:
time: 83.5 us; the launch traced here: 83.4 us
  Pallas kernels  78.9 us (94%)
  local copies, waits for them, and re-layouts  3.14 us (4%)
  between operations  1.29 us (2%)
    pallas_call x1, Pallas kernels, local(): pl.pallas_call(kernel, out_shape=(out, out), in_specs=[hbm] * 8, out_spec...  78.9 us
    unnamed x2, local copies, waits for them, and re-layouts  3.14 us

profile of v4, /device:TPU:1, one launch (start us, length us, event | category | flops | bytes accessed | tf_op | source)
XLA Modules:
  0.0 83.4 jit_solution(14978411585692405964)
XLA Ops:
  1.3 78.9 %lobpcg.1 = (f32[256,128]{1,0:T(8,128)}, f32[256,128]{1,0:T(8,128)}) custom-call(f32[256,128]{1,0:T(8,128)} %x_hbm.1, f32[2,128]{1,0:T(2,128)} %bitcast.5, bf16[64,128,128]{2,1,0:T(8,128)(2,1)} %bitcast.4, s32[1,64]{1,0:T(1,128)} %bitcast.6, s32[1,64]{1,0:T(1,128)} %bitcast.7, s32[1,1]{1,0:T(1,128)S(6)} %copy.12.live_hbm, f32[256,128]{1,0:T(8,128)} %rot1_hbm.1, ...), custom_call_target="tpu_custom_call" | custom-call | tf_op jit(solution)/shard_map/lobpcg/pallas_call | solution.py:433
  80.2 1.6 %copy.13 = f32[256,128]{1,0:T(8,128)} copy(f32[256,128]{1,0:T(8,128)} %get-tuple-element.4) | data formatting | bytes 262144
  81.8 1.6 %copy.14 = f32[256,128]{1,0:T(8,128)} copy(f32[256,128]{1,0:T(8,128)} %get-tuple-element.5) | data formatting | bytes 262144

commit v5 on v4

--- a/solution.py
+++ b/solution.py
@@ -355,15 +355,15 @@
     reduce_start(0, gram_of(x_ref[...], d0), squares(d0))
     gather_middle(2)
     gather_middle(3)
-    reduce_sibling(0)
     gather_end(2)
     multiply(2)
-    reduce_z(0)
+    reduce_sibling(0)
     gather_end(3)
     multiply(3)
+    reduce_z(0)
     scatter_middle(2)
+    scatter_middle(3)
     reduce_share(0)
-    scatter_middle(3)
     next_gather(2)
     next_gather(3)
 

time: 83.5 us -> 82.7 us (level)
  Pallas kernels: 78.9 us -> 78 us
    pallas_call x1, Pallas kernels: 78.9 us -> 78 us  [local(): pl.pallas_call(kernel, out_shape=(out, out), in_specs=[hbm] * 8, out_spec...]
where the time goes in v5:
time: 82.7 us; the launch traced here: 82.4 us
  Pallas kernels  78 us (94%)
  local copies, waits for them, and re-layouts  3.14 us (4%)
  between operations  1.29 us (2%)
    pallas_call x1, Pallas kernels, local(): pl.pallas_call(kernel, out_shape=(out, out), in_specs=[hbm] * 8, out_spec...  78 us
    unnamed x2, local copies, waits for them, and re-layouts  3.14 us

profile of v5, /device:TPU:1, one launch (start us, length us, event | category | flops | bytes accessed | tf_op | source)
XLA Modules:
  0.0 82.4 jit_solution(5352786390695841025)
XLA Ops:
  1.3 78.0 %lobpcg.1 = (f32[256,128]{1,0:T(8,128)}, f32[256,128]{1,0:T(8,128)}) custom-call(f32[256,128]{1,0:T(8,128)} %x_hbm.1, f32[2,128]{1,0:T(2,128)} %bitcast.5, bf16[64,128,128]{2,1,0:T(8,128)(2,1)} %bitcast.4, s32[1,64]{1,0:T(1,128)} %bitcast.6, s32[1,64]{1,0:T(1,128)} %bitcast.7, s32[1,1]{1,0:T(1,128)S(6)} %copy.12.live_hbm, f32[256,128]{1,0:T(8,128)} %rot1_hbm.1, ...), custom_call_target="tpu_custom_call" | custom-call | tf_op jit(solution)/shard_map/lobpcg/pallas_call | solution.py:433
  79.3 1.6 %copy.13 = f32[256,128]{1,0:T(8,128)} copy(f32[256,128]{1,0:T(8,128)} %get-tuple-element.4) | data formatting | bytes 262144
  80.9 1.6 %copy.14 = f32[256,128]{1,0:T(8,128)} copy(f32[256,128]{1,0:T(8,128)} %get-tuple-element.5) | data formatting | bytes 262144
